TPU v7x, 512 devices: a whole 4x8x8 slice. The times are simulated.
512 devices in a mesh: src: 64 (over z_lo, y, core), sub: 8 (over x, z_hi).
Axes of the slice: x: 4, y: 8, z: 8 (z_hi: 2, z_lo: 4; z = z_hi * 4 + z_lo), core: 2. Of those that a mesh axis runs over, the one named last changes fastest.
Arguments:
- child_rhs: float32 [8, 1024, 16384], P('sub', None, 'src'), may hold values from -6 to 6
- root_rhs: float32 [2048, 16384], P('sub', 'src'), may hold values from -6 to 6
- child_inverse: bfloat16 [8, 1024, 1024], P('sub', 'src'), as said below
- coupling_block: bfloat16 [8, 1024, 1024], P('sub', 'src'), may hold values from -0.1875 to 0.1875
- root_inverse: bfloat16 [2048, 2048], P('sub', 'src'), as said below
- child_orders: int32 [8], P('sub'), may hold values from 716 to 1024, as said below
- coupling_rows: int32 [8, 1024], P('sub'), may hold values from 0 to 2047, as said below
Outputs:
- child_solution: float32 [8, 1024, 16384], P('sub', None, 'src')
- root_solution: float32 [2048, 16384], P('sub', 'src')
Inputs may be any that keep to these rules, and one draw needn't show every extreme that they name: Each child_inverse[j] is lower triangular: zero above the diagonal, diagonal entries between 0.8 and 1.25. `root_inverse`: lower triangular: zero above the diagonal, diagonal entries between 0.8 and 1.25. `coupling_rows`: each row holds 1024 distinct root rows in increasing order. `child_orders`: some child has order 1024.
All inputs are finite; a program needn't handle non-finite values.
Results may differ from a plain program's by a relative error of at most 0.0093.
Values may be sent and summed in bfloat16 or wider, within the bound.
No kernel may reach another device: no remote copies, remote signals or barrier semaphores. Data moves between devices by JAX's collectives and lax.ppermute only.
A program may use at most 64 MiB of HBM per device.

v0:
```python
import jax
import jax.numpy as jnp
from jax import lax
from jax.sharding import PartitionSpec as P


def sent_to_all(x, axis):
    length = lax.axis_size(axis)
    return lax.all_to_all(jnp.broadcast_to(x[None], (length, *x.shape)), axis, 0, 0, tiled=True)


def in_order(blocks, dim):
    lengths = list(blocks.shape[1:])
    lengths[dim] *= blocks.shape[0]
    return jnp.moveaxis(blocks, 0, dim).reshape(lengths)


def collect(x, axis, dim):
    blocks = sent_to_all(x, axis)
    return in_order(blocks, dim)


def in_blocks(x, dim, length):
    before, after = (x.shape[:dim], x.shape[dim + 1 :])
    return jnp.moveaxis(x.reshape(*before, length, -1, *after), dim, 0)


def sum_at_owner(x, axis, dim):
    length = lax.axis_size(axis)
    blocks = lax.all_to_all(in_blocks(x, dim, length), axis, 0, 0, tiled=True)
    return jnp.sum(blocks.astype(jnp.float32), axis=0)


def contract_rows(left, right):
    return lax.dot_general(
        left, right, (((0,), (0,)), ((), ())), preferred_element_type=jnp.float32
    )


def on_device(
    child_rhs, root_rhs, child_inverse, coupling_block, root_inverse, child_orders, coupling_rows
):
    inverse = child_inverse[0]
    coupling = coupling_block[0]
    coupling_index = coupling_rows[0]
    columns = child_rhs.shape[2]
    child_order = inverse.shape[1]
    root_order = root_inverse.shape[1] * lax.axis_size("src")
    alive = (lax.iota(jnp.int32, child_order) < child_orders[0])[:, None]
    child_source = jnp.where(alive, child_rhs[0], 0.0).astype(jnp.bfloat16)
    whole_inverse = lax.all_gather(inverse, "src", axis=0, tiled=True)
    whole_coupling = collect(coupling, "src", 0)
    forward = jnp.dot(whole_inverse, child_source, preferred_element_type=jnp.float32)
    child_solved = jnp.where(alive, forward, 0.0)
    solved_round = child_solved.astype(jnp.bfloat16)
    update = jnp.dot(whole_coupling, solved_round, preferred_element_type=jnp.float32)
    placed = jnp.zeros((root_order, columns), jnp.float32).at[coupling_index].add(update)
    share = sum_at_owner(placed.astype(jnp.bfloat16), "sub", 0)
    root_source = collect((root_rhs - share).astype(jnp.bfloat16), "sub", 0)
    root_rows = lax.all_gather(root_inverse, "src", axis=1, tiled=True)
    root_forward = jnp.dot(root_rows, root_source, preferred_element_type=jnp.float32)
    root_round = root_forward.astype(jnp.bfloat16)
    partial_root = contract_rows(root_rows, root_round)
    root_out = sum_at_owner(partial_root.astype(jnp.bfloat16), "sub", 0)
    rounded_all = collect(root_out.astype(jnp.bfloat16), "sub", 0)
    picked = rounded_all[coupling_index]
    pulled = contract_rows(whole_coupling, picked)
    residue = jnp.where(alive, child_solved - pulled, 0.0).astype(jnp.bfloat16)
    backward = contract_rows(whole_inverse, residue)
    child_out = jnp.where(alive, backward, 0.0)[None]
    return (child_out, root_out)


def solution(mesh):
    return jax.shard_map(
        on_device,
        mesh=mesh,
        in_specs=(
            P("sub", None, "src"),
            P("sub", "src"),
            P("sub", "src", None),
            P("sub", "src", None),
            P("sub", "src"),
            P("sub"),
            P("sub", None),
        ),
        out_specs=(P("sub", None, "src"), P("sub", "src")),
        check_vma=False,
    )
```

profile of v0, /device:TPU:73, one launch (start us, length us, event | category | flops | bytes accessed | tf_op | source)
XLA Modules:
  0.0 402.6 jit_solution(723256197187637208)
XLA Ops:
  7.2 0.0 all-gather.6.cloned.1.call-start
  7.2 0.7 all-gather.6.cloned.1.call-update
  7.9 2.3 broadcast_in_dim.62
  10.2 0.0 copy-start.4
  10.2 13.1 %all-to-all-start = ((bf16[64,16,1024]{2,1,0:T(8,128)(2,1)}), bf16[64,16,1024]{2,1,0:T(8,128)(2,1)S(1)}, u32[]{:S(2)}, u32[]{:S(2)}) async-start(bf16[64,16,1024]{2,1,0:T(8,128)(2,1)} %broadcast_in_dim.62), calls=%async_computation | async-start | bytes 4194304 | tf_op jit(solution)/shard_map/all_to_all | solution.py:9
  24.0 0.0 copy-done.4
  24.0 130.5 %all-gather.6.cloned.1.call-done = bf16[1,1024,1024]{2,1,0:T(8,128)(2,1)} async-done(((bf16[1,16,1024]{2,1,0:T(8,128)(2,1)}), bf16[1,1024,1024]{2,1,0:T(8,128)(2,1)}) %all-gather.6.cloned.1.call-update) | async-done | bytes 2097168 | tf_op jit(solution)/shard_map/all_gather | solution.py:51
  154.5 2.9 fusion.4
  157.4 0.0 copy-start.2
  157.4 0.0 all-to-all-done
  157.4 0.0 copy-start
  157.4 2.0 convolution_bitcast_fusion
  159.4 0.0 copy-done.2
  159.4 0.0 copy-done
  159.4 2.6 copy.13
  162.0 7.0 %scatter_custom_fusion = f32[2048,256]{1,0:T(8,128)S(1)} fusion(s32[1024]{0:T(1024)S(1)} %bitcast.50, f32[1024,256]{1,0:T(8,128)} %copy.13, f32[]{:T(128)} %constant.3.clone.1), kind=kCustom, calls=%fused_computation.20 | custom fusion | flops 262144 | bytes 2097664 | tf_op jit(solution)/shard_map/scatter-add | solution.py:57
  169.0 1.1 convert_element_type.42
  170.1 0.0 copy-start.3
  170.1 9.9 %all-to-all-start.1 = ((bf16[8,256,256]{2,1,0:T(8,128)(2,1)}), bf16[8,256,256]{2,1,0:T(8,128)(2,1)S(1)}, u32[]{:S(2)}, u32[]{:S(2)}) async-start(bf16[8,256,256]{2,1,0:T(8,128)(2,1)} %bitcast.8), calls=%async_computation.1 | async-start | bytes 2097152 | tf_op jit(solution)/shard_map/all_to_all | solution.py:30
  180.0 0.0 all-gather.4.cloned.1.call-start
  180.1 0.7 all-gather.4.cloned.1.call-update
  180.8 30.2 %all-to-all-done.1 = bf16[8,256,256]{2,1,0:T(8,128)(2,1)S(1)} async-done(((bf16[8,256,256]{2,1,0:T(8,128)(2,1)}), bf16[8,256,256]{2,1,0:T(8,128)(2,1)S(1)}, u32[]{:S(2)}, u32[]{:S(2)}) %all-to-all-start.1) | async-done | bytes 1048608 | tf_op jit(solution)/shard_map/all_to_all | solution.py:30
  210.9 0.1 convert_reduce_fusion.1
  211.1 0.0 copy-done.3
  211.1 1.1 broadcast_in_dim.63
  212.2 3.6 all-to-all-start.2
  215.8 96.6 %all-gather.4.cloned.1.call-done = bf16[256,2048]{0,1:T(8,128)(2,1)} async-done(((bf16[256,32]{0,1:T(8,128)(2,1)}), bf16[256,2048]{0,1:T(8,128)(2,1)}) %all-gather.4.cloned.1.call-update) | async-done | bytes 1048592 | tf_op jit(solution)/shard_map/all_gather | solution.py:60
  312.4 0.0 all-to-all-done.2
  312.4 2.8 convolution_convert_fusion
  315.2 0.1 copy.22
  315.3 42.1 %all_to_all.25 = bf16[8,256,256]{1,2,0:T(8,128)(2,1)S(1)} all-to-all(bf16[8,256,256]{1,2,0:T(8,128)(2,1)S(1)} %bitcast.46), channel_id=1, replica_groups=mesh['src'=64,'sub'=8] {'sub'}, dimensions={0} | all-to-all | bytes 2097152 | tf_op jit(solution)/shard_map/all_to_all | solution.py:30
  357.4 0.1 convert_reduce_fusion
  357.6 0.1 copy.16
  357.7 1.0 broadcast_in_dim.64
  358.7 3.6 all-to-all-start.4
  362.3 0.8 copy.18
  363.2 22.9 %all-to-all-done.4 = bf16[8,256,256]{2,1,0:T(8,128)(2,1)S(1)} async-done(((bf16[8,256,256]{2,1,0:T(8,128)(2,1)}), bf16[8,256,256]{2,1,0:T(8,128)(2,1)S(1)}, u32[]{:S(2)}, u32[]{:S(2)}) %all-to-all-start.4) | async-done | bytes 1048608 | tf_op jit(solution)/shard_map/all_to_all | solution.py:9
  386.1 0.0 copy-start.1
  386.1 5.0 %gather_fusion = bf16[1024,256]{1,0:T(8,128)(2,1)} fusion(bf16[2048,256]{1,0:T(8,128)(2,1)S(1)} %bitcast.43, s32[1024]{0:T(1024)S(1)} %broadcast_clamp_fusion), kind=kCustom, calls=%fused_computation | custom fusion | bytes 1052672 | tf_op jit(solution)/shard_map/gather | solution.py:66
  391.1 0.0 copy-done.1
  391.1 3.3 fusion.10
  394.4 1.3 copy.17
  (5 shorter events, 0.1 us)
Async XLA Ops:
  7.2 147.3 %all-gather.6.cloned.1.call-start = ((), (), s32[]{:S(2)}) async-start(), calls=%async_computation.6 | async-start | bytes 2129920 | tf_op jit(solution)/shard_map/all_gather | solution.py:51
  10.2 13.7 %copy-start.4 = (s32[1,1024]{1,0:T(1,128)S(1)}, s32[1,1024]{1,0:T(1,128)}, u32[]{:S(2)}) copy-start(s32[1,1024]{1,0:T(1,128)} %param.13) | copy-start | bytes 12292
  10.2 147.2 %all-to-all-start = ((bf16[64,16,1024]{2,1,0:T(8,128)(2,1)}), bf16[64,16,1024]{2,1,0:T(8,128)(2,1)S(1)}, u32[]{:S(2)}, u32[]{:S(2)}) async-start(bf16[64,16,1024]{2,1,0:T(8,128)(2,1)} %broadcast_in_dim.62), calls=%async_computation | async-start | bytes 4194304 | tf_op jit(solution)/shard_map/all_to_all | solution.py:9
  157.4 2.0 copy-start.2
  157.4 2.0 copy-start
  170.1 41.0 %copy-start.3 = (f32[256,256]{1,0:T(8,128)S(1)}, f32[256,256]{1,0:T(8,128)}, u32[]{:S(2)}) copy-start(f32[256,256]{1,0:T(8,128)} %param.8) | copy-start | bytes 786436
  170.1 40.8 %all-to-all-start.1 = ((bf16[8,256,256]{2,1,0:T(8,128)(2,1)}), bf16[8,256,256]{2,1,0:T(8,128)(2,1)S(1)}, u32[]{:S(2)}, u32[]{:S(2)}) async-start(bf16[8,256,256]{2,1,0:T(8,128)(2,1)} %bitcast.8), calls=%async_computation.1 | async-start | bytes 2097152 | tf_op jit(solution)/shard_map/all_to_all | solution.py:30
  180.0 132.4 %all-gather.4.cloned.1.call-start = ((), (), s32[]{:S(2)}) async-start(), calls=%async_computation.5 | async-start | bytes 1064960 | tf_op jit(solution)/shard_map/all_gather | solution.py:60
  212.2 100.2 %all-to-all-start.2 = ((bf16[8,256,256]{2,1,0:T(8,128)(2,1)}), bf16[8,256,256]{2,1,0:T(8,128)(2,1)S(1)}, u32[]{:S(2)}, u32[]{:S(2)}) async-start(bf16[8,256,256]{2,1,0:T(8,128)(2,1)} %broadcast_in_dim.63), calls=%async_computation.2 | async-start | bytes 2097152 | tf_op jit(solution)/shard_map/all_to_all | solution.py:9
  358.7 27.3 %all-to-all-start.4 = ((bf16[8,256,256]{2,1,0:T(8,128)(2,1)}), bf16[8,256,256]{2,1,0:T(8,128)(2,1)S(1)}, u32[]{:S(2)}, u32[]{:S(2)}) async-start(bf16[8,256,256]{2,1,0:T(8,128)(2,1)} %broadcast_in_dim.64), calls=%async_computation.4 | async-start | bytes 2097152 | tf_op jit(solution)/shard_map/all_to_all | solution.py:9
  386.1 5.0 %copy-start.1 = (bf16[64,16,1024]{2,1,0:T(8,128)(2,1)S(1)}, bf16[64,16,1024]{2,1,0:T(8,128)(2,1)}, u32[]{:S(2)}) copy-start(bf16[64,16,1024]{2,1,0:T(8,128)(2,1)} %copy-done) | copy-start | bytes 6291460
Sparse Core Ops, SparseCore 0:
  10.1 144.2 all-gather.5
  183.0 129.3 all-gather.3
where the time goes:
time: 403 us
  waiting for transfers between devices  282 us (70%)
  blocking collectives  42.1 us (10%)
  starting transfers between devices  30.2 us (7%)
  between operations  14.8 us (4%)
  local copies, waits for them, and re-layouts  14.3 us (4%)
  matrix products  11 us (3%)
  other arithmetic  8.5 us (2%)
    all_gather x1, waiting for transfers between devices, on_device(): whole_inverse = lax.all_gather(inverse, 'src', axis=0, tiled=True)  130 us
    all_gather x1, waiting for transfers between devices, on_device(): root_rows = lax.all_gather(root_inverse, 'src', axis=1, tiled=True)  96.6 us
    all_to_all x1, blocking collectives, sum_at_owner(): blocks = lax.all_to_all(in_blocks(x, dim, length), axis, 0, 0, tiled=True)  42.1 us
    all_to_all x1, waiting for transfers between devices, sum_at_owner(): blocks = lax.all_to_all(in_blocks(x, dim, length), axis, 0, 0, tiled=True)  30.2 us
    all_to_all x3, waiting for transfers between devices, sent_to_all(): lax.all_to_all(jnp.broadcast_to(x[None], (length, *x.shape)), axis, 0, 0,...  22.9 us
    all_to_all x3, starting transfers between devices, sent_to_all(): lax.all_to_all(jnp.broadcast_to(x[None], (length, *x.shape)), axis, 0, 0,...  20.2 us
    all_to_all x1, starting transfers between devices, sum_at_owner(): blocks = lax.all_to_all(in_blocks(x, dim, length), axis, 0, 0, tiled=True)  9.91 us
  transfers between devices with their start and end apart: 6, of which 4 were waited for; matrix products, arithmetic and copies ran while one was open for 2% of the time, Pallas kernels for 0%

commit v1 on v0

--- a/solution.py
+++ b/solution.py
@@ -57,7 +57,9 @@
     placed = jnp.zeros((root_order, columns), jnp.float32).at[coupling_index].add(update)
     share = sum_at_owner(placed.astype(jnp.bfloat16), "sub", 0)
     root_source = collect((root_rhs - share).astype(jnp.bfloat16), "sub", 0)
-    root_rows = lax.all_gather(root_inverse, "src", axis=1, tiled=True)
+    root_rows = jnp.concatenate(
+        lax.all_to_all(jnp.stack([root_inverse] * lax.axis_size("src")), "src", 0, 0), axis=1
+    )
     root_forward = jnp.dot(root_rows, root_source, preferred_element_type=jnp.float32)
     root_round = root_forward.astype(jnp.bfloat16)
     partial_root = contract_rows(root_rows, root_round)

time: 403 us -> 358 us (0.89)
  waiting for transfers between devices: 282 us -> 181 us
  blocking collectives: 42.1 us -> 105 us
  starting transfers between devices: 30.2 us -> 24.6 us
    all_gather x1 -> x0, waiting for transfers between devices: 96.6 us -> none  [on_device(): root_rows = lax.all_gather(root_inverse, 'src', axis=1, tiled=True)]
    all_to_all x0 -> x1, blocking collectives: none -> 33.5 us  [sent_to_all(): lax.all_to_all(jnp.broadcast_to(x[None], (length, *x.shape)), axis, 0, 0,...]
    all_to_all x1 -> x2, blocking collectives: 42.1 us -> 71.2 us  [sum_at_owner(): blocks = lax.all_to_all(in_blocks(x, dim, length), axis, 0, 0, tiled=True)]
    all_to_all x3 -> x2, starting transfers between devices: 20.2 us -> 16.6 us  [sent_to_all(): lax.all_to_all(jnp.broadcast_to(x[None], (length, *x.shape)), axis, 0, 0,...]
    all_to_all x3 -> x2, waiting for transfers between devices: 22.9 us -> 22.9 us  [sent_to_all(): lax.all_to_all(jnp.broadcast_to(x[None], (length, *x.shape)), axis, 0, 0,...]
  transfers between devices with their start and end apart: 6 -> 4, of which waited for: 4 -> 3; matrix products, arithmetic and copies ran while one was open for 2% -> 2% of each run, Pallas kernels for 0% -> 0%
where the time goes in v1:
time: 358 us; the launch traced here: 357 us
  waiting for transfers between devices  181 us (51%)
  blocking collectives  105 us (29%)
  starting transfers between devices  24.6 us (7%)
  between operations  14.9 us (4%)
  local copies, waits for them, and re-layouts  14.4 us (4%)
  matrix products  9.52 us (3%)
  other arithmetic  7.49 us (2%)
    all_gather x1, waiting for transfers between devices, on_device(): whole_inverse = lax.all_gather(inverse, 'src', axis=0, tiled=True)  131 us
    all_to_all x2, blocking collectives, sum_at_owner(): blocks = lax.all_to_all(in_blocks(x, dim, length), axis, 0, 0, tiled=True)  71.2 us
    all_to_all x1, blocking collectives, sent_to_all(): lax.all_to_all(jnp.broadcast_to(x[None], (length, *x.shape)), axis, 0, 0,...  33.5 us
    all_to_all x1, waiting for transfers between devices, on_device(): lax.all_to_all(jnp.stack([root_inverse] * lax.axis_size('src')), 'src', 0...  27.3 us
    all_to_all x2, waiting for transfers between devices, sent_to_all(): lax.all_to_all(jnp.broadcast_to(x[None], (length, *x.shape)), axis, 0, 0,...  22.9 us
    all_to_all x2, starting transfers between devices, sent_to_all(): lax.all_to_all(jnp.broadcast_to(x[None], (length, *x.shape)), axis, 0, 0,...  16.6 us
    all_to_all x1, starting transfers between devices, on_device(): lax.all_to_all(jnp.stack([root_inverse] * lax.axis_size('src')), 'src', 0...  7.9 us
  transfers between devices with their start and end apart: 4, of which 3 were waited for; matrix products, arithmetic and copies ran while one was open for 2% of the time, Pallas kernels for 0%

profile of v1, /device:TPU:73, one launch (start us, length us, event | category | flops | bytes accessed | tf_op | source)
XLA Modules:
  0.0 356.9 jit_solution(7640826835358834427)
XLA Ops:
  7.2 0.0 all-gather.3.cloned.1.call-start
  7.2 0.7 all-gather.3.cloned.1.call-update
  7.9 2.3 broadcast_in_dim.62
  10.2 0.0 copy-start.5
  10.2 13.1 %all-to-all-start = ((bf16[64,16,1024]{2,1,0:T(8,128)(2,1)}), bf16[64,16,1024]{2,1,0:T(8,128)(2,1)S(1)}, u32[]{:S(2)}, u32[]{:S(2)}) async-start(bf16[64,16,1024]{2,1,0:T(8,128)(2,1)} %broadcast_in_dim.62), calls=%async_computation | async-start | bytes 4194304 | tf_op jit(solution)/shard_map/all_to_all | solution.py:9
  24.0 0.0 copy-done.5
  24.0 130.6 %all-gather.3.cloned.1.call-done = bf16[1,1024,1024]{2,1,0:T(8,128)(2,1)} async-done(((bf16[1,16,1024]{2,1,0:T(8,128)(2,1)}), bf16[1,1024,1024]{2,1,0:T(8,128)(2,1)}) %all-gather.3.cloned.1.call-update) | async-done | bytes 2097168 | tf_op jit(solution)/shard_map/all_gather | solution.py:51
  154.6 2.9 fusion.4
  157.5 0.0 copy-start.2
  157.5 0.0 all-to-all-done
  157.5 0.0 copy-start
  157.5 2.0 convolution_bitcast_fusion
  159.5 0.0 copy-done.2
  159.5 0.0 copy-done
  159.5 2.6 copy.14
  162.0 7.0 %scatter_custom_fusion = f32[2048,256]{1,0:T(8,128)S(1)} fusion(s32[1024]{0:T(1024)S(1)} %bitcast.55, f32[1024,256]{1,0:T(8,128)} %copy.14, f32[]{:T(128)} %constant.3.clone.1), kind=kCustom, calls=%fused_computation.20 | custom fusion | flops 262144 | bytes 2097664 | tf_op jit(solution)/shard_map/scatter-add | solution.py:57
  169.1 0.0 copy-start.4
  169.1 0.1 convert_element_type.42
  169.2 39.7 %all_to_all.30 = bf16[8,256,256]{2,1,0:T(8,128)(2,1)S(1)} all-to-all(bf16[8,256,256]{2,1,0:T(8,128)(2,1)S(1)} %bitcast.50), channel_id=1, replica_groups=mesh['src'=64,'sub'=8] {'sub'}, dimensions={0} | all-to-all | bytes 2097152 | tf_op jit(solution)/shard_map/all_to_all | solution.py:30
  208.9 0.0 copy-done.4
  208.9 0.0 copy-start.3
  208.9 1.1 stack.2
  210.0 7.9 %all-to-all-start.3 = ((bf16[64,256,32]{1,2,0:T(8,128)(2,1)}), bf16[64,256,32]{1,2,0:T(8,128)(2,1)S(1)}, u32[]{:S(2)}, u32[]{:S(2)}) async-start(bf16[64,256,32]{1,2,0:T(8,128)(2,1)} %stack.2), calls=%async_computation.3 | async-start | bytes 2097152 | tf_op jit(solution)/shard_map/all_to_all | solution.py:61
  217.9 0.1 convert_reduce_fusion.1
  218.1 0.0 copy-done.3
  218.1 27.3 %all-to-all-done.3 = bf16[64,256,32]{1,2,0:T(8,128)(2,1)S(1)} async-done(((bf16[64,256,32]{1,2,0:T(8,128)(2,1)}), bf16[64,256,32]{1,2,0:T(8,128)(2,1)S(1)}, u32[]{:S(2)}, u32[]{:S(2)}) %all-to-all-start.3) | async-done | bytes 1048608 | tf_op jit(solution)/shard_map/all_to_all | solution.py:61
  245.4 0.1 broadcast_in_dim.63
  245.5 33.5 %all_to_all.31 = bf16[8,256,256]{2,1,0:T(8,128)(2,1)S(1)} all-to-all(bf16[8,256,256]{2,1,0:T(8,128)(2,1)S(1)} %broadcast_in_dim.63), channel_id=1, replica_groups=mesh['src'=64,'sub'=8] {'sub'}, dimensions={0} | all-to-all | bytes 2097152 | tf_op jit(solution)/shard_map/all_to_all | solution.py:9
  279.0 1.3 convolution_convert_fusion
  280.3 0.1 copy.23
  280.4 31.5 %all_to_all.32 = bf16[8,256,256]{1,2,0:T(8,128)(2,1)S(1)} all-to-all(bf16[8,256,256]{1,2,0:T(8,128)(2,1)S(1)} %bitcast.51), channel_id=1, replica_groups=mesh['src'=64,'sub'=8] {'sub'}, dimensions={0} | all-to-all | bytes 2097152 | tf_op jit(solution)/shard_map/all_to_all | solution.py:30
  311.8 0.1 convert_reduce_fusion
  312.0 0.1 copy.17
  312.1 1.0 broadcast_in_dim.64
  313.1 3.6 all-to-all-start.5
  316.7 0.8 copy.19
  317.5 22.9 %all-to-all-done.5 = bf16[8,256,256]{2,1,0:T(8,128)(2,1)S(1)} async-done(((bf16[8,256,256]{2,1,0:T(8,128)(2,1)}), bf16[8,256,256]{2,1,0:T(8,128)(2,1)S(1)}, u32[]{:S(2)}, u32[]{:S(2)}) %all-to-all-start.5) | async-done | bytes 1048608 | tf_op jit(solution)/shard_map/all_to_all | solution.py:9
  340.4 0.0 copy-start.1
  340.5 5.0 %gather_fusion = bf16[1024,256]{1,0:T(8,128)(2,1)} fusion(bf16[2048,256]{1,0:T(8,128)(2,1)S(1)} %bitcast.46, s32[1024]{0:T(1024)S(1)} %broadcast_clamp_fusion), kind=kCustom, calls=%fused_computation | custom fusion | bytes 1052672 | tf_op jit(solution)/shard_map/gather | solution.py:68
  345.4 0.0 copy-done.1
  345.4 3.3 fusion.10
  348.8 1.3 copy.18
  (5 shorter events, 0.1 us)
Async XLA Ops:
  7.2 147.4 %all-gather.3.cloned.1.call-start = ((), (), s32[]{:S(2)}) async-start(), calls=%async_computation.6 | async-start | bytes 2129920 | tf_op jit(solution)/shard_map/all_gather | solution.py:51
  10.2 13.7 %copy-start.5 = (s32[1,1024]{1,0:T(1,128)S(1)}, s32[1,1024]{1,0:T(1,128)}, u32[]{:S(2)}) copy-start(s32[1,1024]{1,0:T(1,128)} %param.13) | copy-start | bytes 12292
  10.2 147.3 %all-to-all-start = ((bf16[64,16,1024]{2,1,0:T(8,128)(2,1)}), bf16[64,16,1024]{2,1,0:T(8,128)(2,1)S(1)}, u32[]{:S(2)}, u32[]{:S(2)}) async-start(bf16[64,16,1024]{2,1,0:T(8,128)(2,1)} %broadcast_in_dim.62), calls=%async_computation | async-start | bytes 4194304 | tf_op jit(solution)/shard_map/all_to_all | solution.py:9
  157.5 2.0 copy-start.2
  157.5 2.0 copy-start
  169.1 39.8 %copy-start.4 = (bf16[256,32]{0,1:T(8,128)(2,1)S(1)}, bf16[256,32]{0,1:T(8,128)(2,1)}, u32[]{:S(2)}) copy-start(bf16[256,32]{0,1:T(8,128)(2,1)} %param.11) | copy-start | bytes 49156
  208.9 9.2 %copy-start.3 = (f32[256,256]{1,0:T(8,128)S(1)}, f32[256,256]{1,0:T(8,128)}, u32[]{:S(2)}) copy-start(f32[256,256]{1,0:T(8,128)} %param.8) | copy-start | bytes 786436
  210.0 35.4 %all-to-all-start.3 = ((bf16[64,256,32]{1,2,0:T(8,128)(2,1)}), bf16[64,256,32]{1,2,0:T(8,128)(2,1)S(1)}, u32[]{:S(2)}, u32[]{:S(2)}) async-start(bf16[64,256,32]{1,2,0:T(8,128)(2,1)} %stack.2), calls=%async_computation.3 | async-start | bytes 2097152 | tf_op jit(solution)/shard_map/all_to_all | solution.py:61
  313.1 27.3 %all-to-all-start.5 = ((bf16[8,256,256]{2,1,0:T(8,128)(2,1)}), bf16[8,256,256]{2,1,0:T(8,128)(2,1)S(1)}, u32[]{:S(2)}, u32[]{:S(2)}) async-start(bf16[8,256,256]{2,1,0:T(8,128)(2,1)} %broadcast_in_dim.64), calls=%async_computation.5 | async-start | bytes 2097152 | tf_op jit(solution)/shard_map/all_to_all | solution.py:9
  340.4 5.0 %copy-start.1 = (bf16[64,16,1024]{2,1,0:T(8,128)(2,1)S(1)}, bf16[64,16,1024]{2,1,0:T(8,128)(2,1)}, u32[]{:S(2)}) copy-start(bf16[64,16,1024]{2,1,0:T(8,128)(2,1)} %copy-done) | copy-start | bytes 6291460
Sparse Core Ops, SparseCore 0:
  10.1 144.3 all-gather.2
